TPU v7x, 32 devices: a whole 2x2x4 slice. The times are simulated.
32 devices in a mesh: st: 8 (over z, x), gr: 4 (over y, core).
Axes of the slice: x: 2, y: 2, z: 4, core: 2. Of those that a mesh axis runs over, the one named last changes fastest.
Arguments:
- states: float32 [32, 24, 768], P(('st', 'gr')), may hold values from -6 to 6
- regions: int32 [24, 768], replicated, may hold values from 0 to 7
- pot_table: float32 [8], replicated, may hold values from -3 to 0
- subspace: bfloat16 [32, 32], P(None, 'st'), may hold values from -1.5 to 1.5
- state_order: int32 [32], replicated, may hold values from 0 to 31, each once
Outputs:
- rotated: bfloat16 [32, 24, 768], P('st', 'gr')
Inputs may be any that keep to these rules, and one draw needn't show every extreme that they name: state_order is a permutation of the window positions.
All inputs are finite; a program needn't handle non-finite values.
Results may differ from a plain program's by a relative error of at most 0.0049.
Values may be sent and summed in bfloat16 or wider, within the bound.
No kernel may reach another device: no remote copies, remote signals or barrier semaphores. Data moves between devices by JAX's collectives and lax.ppermute only.
A program may use at most 64 MiB of HBM per device.

v0:
```python
import jax
import jax.numpy as jnp
from jax import lax
from jax.sharding import PartitionSpec as P

NY = 24
NZ = 32
DEG = 4
coef_center = -5369.0 / 1800.0
coef_list = (12.0 / 7.0, -15.0 / 56.0, 10.0 / 189.0, -1.0 / 112.0, 2.0 / 1925.0, -1.0 / 16632.0)
centre = 6.75
half_width = 5.25


def shift_cols(field, offset):
    width = field.shape[1]
    if offset > 0:
        return jnp.pad(field[:, offset:], ((0, 0), (0, offset)))
    return jnp.pad(field[:, : width + offset], ((0, 0), (-offset, 0)))


def shift_rows(field, offset):
    height = field.shape[0]
    if offset > 0:
        return jnp.pad(field[offset:, :], ((0, offset), (0, 0)))
    return jnp.pad(field[: height + offset, :], ((-offset, 0), (0, 0)))


def laplace(field):
    zpos = lax.broadcasted_iota(jnp.int32, field.shape, 1) % NZ
    total = 3.0 * coef_center * field
    for step in range(1, 7):
        xpair = shift_rows(field, step) + shift_rows(field, -step)
        ypair = shift_cols(field, step * NZ) + shift_cols(field, -step * NZ)
        zplus = jnp.where(zpos + step < NZ, shift_cols(field, step), 0.0)
        zminus = jnp.where(zpos - step >= 0, shift_cols(field, -step), 0.0)
        total = total + coef_list[step - 1] * (xpair + ypair + (zplus + zminus))
    return total


def shifted_op(field, potential):
    return -0.5 * laplace(field) + potential * field - centre * field


def lookup(regions, pot_table):
    levels = lax.broadcasted_iota(jnp.int32, (pot_table.shape[0], 1, 1), 0)
    hits = regions[None, :, :] == levels
    return jnp.sum(jnp.where(hits, pot_table[:, None, None], 0.0), axis=0)


def per_device(states, regions, pot_table, subspace, state_order):
    potential = lookup(regions, pot_table)
    previous = states[0]
    current = shifted_op(previous, potential) * (1.0 / half_width)
    for step in range(1, DEG):
        following = shifted_op(current, potential) * (2.0 / half_width) - previous
        previous = current
        current = following
    filtered = current.astype(jnp.bfloat16)
    groups = lax.axis_size("gr")
    weights = jnp.take(subspace, state_order, axis=0)
    columns = weights.shape[1]
    blocks = lax.all_to_all(filtered[None], "gr", split_axis=1, concat_axis=0, tiled=True)
    slab_rows = blocks.shape[1]
    flat_blocks = blocks.reshape(groups, slab_rows * NY * NZ)
    summed = lax.dot_general(
        weights,
        lax.all_gather(flat_blocks, "st", axis=0, tiled=True),
        (((0,), (0,)), ((), ())),
        preferred_element_type=jnp.float32,
    )
    return summed.reshape(columns, slab_rows, NY * NZ).astype(jnp.bfloat16)


def solution(mesh):
    in_specs = (P(("st", "gr"), None, None), P(), P(), P(None, "st"), P())
    out_specs = P("st", "gr", None)
    return jax.shard_map(
        per_device, mesh=mesh, in_specs=in_specs, out_specs=out_specs, check_vma=False
    )
```

profile of v0, /device:TPU:0, one launch (start us, length us, event | category | flops | bytes accessed | tf_op | source)
XLA Modules:
  0.0 51.4 jit_solution(2509546299188329413)
XLA Ops:
  0.0 1.1 %fusion.75 = (f32[24,736]{1,0:T(8,128)S(1)}, f32[24,736]{1,0:T(8,128)S(1)}) fusion(f32[24,768]{1,0:T(8,128)} %bitcast.37), kind=kLoop, calls=%fused_computation.112 | loop fusion | bytes 282624 | tf_op jit(solution)/shard_map/slice | solution.py:18
  1.1 0.1 fusion.76
  1.2 0.1 fusion.77
  1.3 0.1 fusion.78
  1.3 0.1 fusion.79
  1.4 0.1 fusion.80
  1.5 0.1 fusion.82
  1.6 0.1 fusion.84
  1.7 0.1 fusion.86
  1.9 0.1 fusion.85
  2.1 0.8 %copy-done.1 = s32[24,768]{1,0:T(8,128)S(1)} copy-done((s32[24,768]{1,0:T(8,128)S(1)}, s32[24,768]{1,0:T(8,128)}, u32[]{:S(2)}) %copy-start.1) | copy-done | bytes 73752
  3.0 0.1 select_reduce_fusion
  3.1 0.4 broadcast_multiply_fusion
  3.5 0.1 fusion.68
  3.7 0.1 fusion.71
  3.8 0.1 fusion.74
  3.9 0.1 fusion.58
  3.9 0.1 fusion.59
  4.1 0.1 fusion.61
  4.1 0.1 fusion.62
  4.3 0.1 fusion.64
  4.3 0.1 fusion.65
  4.5 0.1 fusion.73
  4.6 0.4 multiply_subtract_fusion.1
  5.1 0.1 fusion.40
  5.2 0.1 fusion.41
  5.3 0.1 fusion.43
  5.4 0.1 fusion.44
  5.5 0.1 fusion.46
  5.5 0.1 fusion.47
  6.1 0.1 fusion.55
  6.1 0.4 multiply_subtract_fusion
  6.7 0.1 fusion.23
  6.9 0.1 fusion.26
  7.0 0.1 fusion.29
  7.6 0.1 fusion.37
  7.7 0.4 fusion.12
  8.2 0.5 broadcast.651
  8.7 0.8 %reduce.2 = bf16[24,768]{1,0:T(8,128)(2,1)S(1)} reduce(bf16[24,1,768]{2,1,0:T(2,128)(2,1)S(1)} %bitcast.49, bf16[]{:T(256)} %broadcast.651), dimensions={1}, to_apply=%bitcast.36.reduce_sub_computation | reduce | bytes 73730
  9.5 0.6 %reshape.42 = bf16[4,2,2304]{2,1,0:T(2,128)(2,1)} reshape(bf16[24,768]{1,0:T(8,128)(2,1)S(1)} %reduce.2) | data formatting | bytes 73728
  10.2 4.4 %all-to-all-start = ((bf16[4,2,2304]{2,1,0:T(2,128)(2,1)}), bf16[4,2,2304]{2,1,0:T(2,128)(2,1)S(1)}, u32[]{:S(2)}, u32[]{:S(2)}) async-start(bf16[4,2,2304]{2,1,0:T(2,128)(2,1)} %reshape.42), calls=%async_computation | async-start | bytes 73728 | tf_op jit(solution)/shard_map/all_to_all | solution.py:63
  14.6 0.7 %copy-done.2 = bf16[32,4]{0,1:T(4,128)(2,1)S(1)} copy-done((bf16[32,4]{0,1:T(4,128)(2,1)S(1)}, bf16[32,4]{0,1:T(4,128)(2,1)}, u32[]{:S(2)}) %copy-start.2) | copy-done | bytes 280
  15.3 0.1 copy.15
  15.4 0.6 %gather_fusion = bf16[32,4]{1,0:T(8,128)(2,1)S(1)} fusion(bf16[32,4]{1,0:T(8,128)(2,1)S(1)} %copy.15, s32[1024]{0:T(1024)S(1)} %pad_clamp_fusion), kind=kCustom, calls=%fused_computation | custom fusion | bytes 640 | tf_op jit(solution)/shard_map/jit(_take)/gather | solution.py:61
  16.0 2.6 %all-to-all-done = bf16[4,2,2304]{2,1,0:T(2,128)(2,1)S(1)} async-done(((bf16[4,2,2304]{2,1,0:T(2,128)(2,1)}), bf16[4,2,2304]{2,1,0:T(2,128)(2,1)S(1)}, u32[]{:S(2)}, u32[]{:S(2)}) %all-to-all-start) | async-done | bytes 36896 | tf_op jit(solution)/shard_map/all_to_all | solution.py:63
  18.6 0.2 bitcast_reduce_fusion
  18.8 31.6 %all-gather = bf16[8,4,4608]{2,1,0:T(4,128)(2,1)S(1)} all-gather(bf16[1,4,4608]{2,1,0:T(4,128)(2,1)S(1)} %reshape.38), channel_id=1, replica_groups=mesh['st'=8,'gr'=4] {'st'}, dimensions={0}, use_global_device_ids=true | all-gather | bytes 331776 | tf_op jit(solution)/shard_map/all_gather | solution.py:68
  50.5 0.9 %convolution_convert_fusion = bf16[4,4608]{1,0:T(4,128)(2,1)} fusion(bf16[32,4608]{1,0:T(8,128)(2,1)S(1)} %reshape.39, bf16[32,4]{1,0:T(8,128)(2,1)S(1)} %gather_fusion, pred[32]{0:T(512)(128)(4,1)S(1)} %compare_and_fusion), kind=kOutput, calls=%fused_computation.1 | convolution fusion | flops 1198208 | bytes 332064 | tf_op jit(solution)/shard_map/dot_general | solution.py:66
  (58 shorter events, 1.7 us)
Async XLA Ops:
  0.0 1.1 %copy-start = (f32[1,24,768]{2,1,0:T(8,128)S(1)}, f32[1,24,768]{2,1,0:T(8,128)}, u32[]{:S(2)}) copy-start(f32[1,24,768]{2,1,0:T(8,128)} %param.5) | copy-start | bytes 221188
  2.1 0.9 %copy-start.1 = (s32[24,768]{1,0:T(8,128)S(1)}, s32[24,768]{1,0:T(8,128)}, u32[]{:S(2)}) copy-start(s32[24,768]{1,0:T(8,128)} %param.6) | copy-start | bytes 221188
  2.1 0.9 %copy-start.3 = (f32[8]{0:T(128)S(1)}, f32[8]{0:T(128)}, u32[]{:S(2)}) copy-start(f32[8]{0:T(128)} %param.7) | copy-start | bytes 100
  10.2 4.4 %copy-start.4 = (s32[32]{0:T(128)S(1)}, s32[32]{0:T(128)}, u32[]{:S(2)}) copy-start(s32[32]{0:T(128)} %param.9) | copy-start | bytes 388
  10.2 8.4 %all-to-all-start = ((bf16[4,2,2304]{2,1,0:T(2,128)(2,1)}), bf16[4,2,2304]{2,1,0:T(2,128)(2,1)S(1)}, u32[]{:S(2)}, u32[]{:S(2)}) async-start(bf16[4,2,2304]{2,1,0:T(2,128)(2,1)} %reshape.42), calls=%async_computation | async-start | bytes 73728 | tf_op jit(solution)/shard_map/all_to_all | solution.py:63
  14.6 0.7 %copy-start.2 = (bf16[32,4]{0,1:T(4,128)(2,1)S(1)}, bf16[32,4]{0,1:T(4,128)(2,1)}, u32[]{:S(2)}) copy-start(bf16[32,4]{0,1:T(4,128)(2,1)} %param.8) | copy-start | bytes 772
where the time goes:
time: 51.7 us; the launch traced here: 51.4 us
  blocking collectives  31.6 us (61%)
  local copies, waits for them, and re-layouts  8.8 us (17%)
  starting transfers between devices  4.4 us (9%)
  other arithmetic  2.71 us (5%)
  waiting for transfers between devices  2.57 us (5%)
  matrix products  0.91 us (2%)
    all_gather x1, blocking collectives, per_device(): lax.all_gather(flat_blocks, 'st', axis=0, tiled=True)  31.6 us
    slice x48, local copies, waits for them, and re-layouts, shift_cols(): return jnp.pad(field[:, offset:], ((0, 0), (0, offset)))  4.65 us
    all_to_all x1, starting transfers between devices, per_device(): lax.all_to_all(filtered[None], 'gr', split_axis=1, concat_axis=0, tiled=T...  4.4 us
    unnamed x16, local copies, waits for them, and re-layouts  2.9 us
    all_to_all x1, waiting for transfers between devices, per_device(): lax.all_to_all(filtered[None], 'gr', split_axis=1, concat_axis=0, tiled=T...  2.57 us
  transfers between devices with their start and end apart: 1, of which 1 were waited for; matrix products, arithmetic and copies ran while one was open for 1% of the time, Pallas kernels for 0%

commit v1 on v0

--- a/solution.py
+++ b/solution.py
@@ -10,6 +10,27 @@
 coef_list = (12.0 / 7.0, -15.0 / 56.0, 10.0 / 189.0, -1.0 / 112.0, 2.0 / 1925.0, -1.0 / 16632.0)
 centre = 6.75
 half_width = 5.25
+
+
+def ring_gather(value, axis, dim):
+    peers, place, rows = (lax.axis_size(axis), lax.axis_index(axis), value.shape[dim])
+    ahead = [(i, (i + 1) % peers) for i in range(peers)]
+    left = [(i, (i - 1) % peers) for i in range(peers)]
+    out = jnp.zeros((*value.shape[:dim], peers * rows, *value.shape[dim + 1 :]), value.dtype)
+    out = lax.dynamic_update_slice_in_dim(out, value, place * rows, axis=dim)
+    from_left = from_right = value
+    halfway = peers // 2
+    for step in range(1, halfway + 1):
+        from_left = lax.ppermute(from_left, axis, ahead)
+        out = lax.dynamic_update_slice_in_dim(
+            out, from_left, (place - step) % peers * rows, axis=dim
+        )
+        if step < peers - halfway:
+            from_right = lax.ppermute(from_right, axis, left)
+            out = lax.dynamic_update_slice_in_dim(
+                out, from_right, (place + step) % peers * rows, axis=dim
+            )
+    return out
 
 
 def shift_cols(field, offset):
@@ -65,7 +86,7 @@
     flat_blocks = blocks.reshape(groups, slab_rows * NY * NZ)
     summed = lax.dot_general(
         weights,
-        lax.all_gather(flat_blocks, "st", axis=0, tiled=True),
+        ring_gather(flat_blocks, "st", 0),
         (((0,), (0,)), ((), ())),
         preferred_element_type=jnp.float32,
     )

time: 51.7 us -> 47 us (0.909)
  blocking collectives: 31.6 us -> 0 us
  starting transfers between devices: 4.4 us -> 19.1 us
  waiting for transfers between devices: 2.57 us -> 14.4 us
    all_gather x1 -> x0, blocking collectives: 31.6 us -> none  [per_device(): lax.all_gather(flat_blocks, 'st', axis=0, tiled=True)]
    ppermute x0 -> x7, starting transfers between devices: none -> 14.7 us  [the longest x3 12.7 us: ring_gather(): from_right = lax.ppermute(from_right, axis, left)]
    ppermute x0 -> x7, waiting for transfers between devices: none -> 12 us  [the longest x4 12 us: ring_gather(): from_left = lax.ppermute(from_left, axis, ahead)]
    unnamed x16 -> x14, local copies, waits for them, and re-layouts: 2.9 us -> 2.82 us
  transfers between devices with their start and end apart: 1 -> 8, of which waited for: 1 -> 5; matrix products, arithmetic and copies ran while one was open for 1% -> 2% of each run, Pallas kernels for 0% -> 0%
where the time goes in v1:
time: 47 us; the launch traced here: 46.7 us
  starting transfers between devices  19.1 us (41%)
  waiting for transfers between devices  14.4 us (31%)
  local copies, waits for them, and re-layouts  9.01 us (19%)
  other arithmetic  2.71 us (6%)
  matrix products  0.91 us (2%)
  between operations  0.56 us (1%)
    ppermute x3, starting transfers between devices, ring_gather(): from_right = lax.ppermute(from_right, axis, left)  12.7 us
    ppermute x4, waiting for transfers between devices, ring_gather(): from_left = lax.ppermute(from_left, axis, ahead)  12 us
    slice x48, local copies, waits for them, and re-layouts, shift_cols(): return jnp.pad(field[:, offset:], ((0, 0), (0, offset)))  4.65 us
    all_to_all x1, starting transfers between devices, per_device(): lax.all_to_all(filtered[None], 'gr', split_axis=1, concat_axis=0, tiled=T...  4.4 us
    unnamed x14, local copies, waits for them, and re-layouts  2.82 us
    all_to_all x1, waiting for transfers between devices, per_device(): lax.all_to_all(filtered[None], 'gr', split_axis=1, concat_axis=0, tiled=T...  2.44 us
    ppermute x4, starting transfers between devices, ring_gather(): from_left = lax.ppermute(from_left, axis, ahead)  2 us
  transfers between devices with their start and end apart: 8, of which 5 were waited for; matrix products, arithmetic and copies ran while one was open for 2% of the time, Pallas kernels for 0%

profile of v1, /device:TPU:0, one launch (start us, length us, event | category | flops | bytes accessed | tf_op | source)
XLA Modules:
  0.0 46.7 jit_solution(6913393524318438423)
XLA Ops:
  0.0 1.1 %fusion.75 = (f32[24,736]{1,0:T(8,128)S(1)}, f32[24,736]{1,0:T(8,128)S(1)}) fusion(f32[24,768]{1,0:T(8,128)} %bitcast.37), kind=kLoop, calls=%fused_computation.120 | loop fusion | bytes 282624 | tf_op jit(solution)/shard_map/slice | solution.py:39
  1.1 0.1 fusion.76
  1.2 0.1 fusion.77
  1.3 0.1 fusion.78
  1.3 0.1 fusion.79
  1.4 0.1 fusion.80
  1.5 0.1 fusion.82
  1.6 0.1 fusion.84
  1.7 0.1 fusion.86
  1.9 0.1 fusion.85
  2.1 0.8 %copy-done.1 = s32[24,768]{1,0:T(8,128)S(1)} copy-done((s32[24,768]{1,0:T(8,128)S(1)}, s32[24,768]{1,0:T(8,128)}, u32[]{:S(2)}) %copy-start.1) | copy-done | bytes 73752
  3.0 0.1 select_reduce_fusion
  3.1 0.4 broadcast_multiply_fusion
  3.5 0.1 fusion.68
  3.7 0.1 fusion.71
  3.9 0.1 fusion.59
  4.1 0.1 fusion.62
  4.3 0.1 fusion.65
  4.5 0.1 fusion.73
  4.6 0.4 multiply_subtract_fusion.1
  5.2 0.1 fusion.41
  5.4 0.1 fusion.44
  5.5 0.1 fusion.47
  6.1 0.1 fusion.55
  6.1 0.4 multiply_subtract_fusion
  6.7 0.1 fusion.23
  6.9 0.1 fusion.26
  7.0 0.1 fusion.29
  7.6 0.1 fusion.37
  7.7 0.4 fusion.12
  8.2 0.5 %broadcast.658 = bf16[]{:T(256)} broadcast(bf16[]{:T(256)} %constant.517), dimensions={} | broadcast | bytes 4
  8.7 0.8 %reduce.2 = bf16[24,768]{1,0:T(8,128)(2,1)S(1)} reduce(bf16[24,1,768]{2,1,0:T(2,128)(2,1)S(1)} %bitcast.49, bf16[]{:T(256)} %broadcast.658), dimensions={1}, to_apply=%bitcast.36.reduce_sub_computation | reduce | bytes 73730
  9.5 0.6 %reshape.39 = bf16[4,2,2304]{2,1,0:T(2,128)(2,1)} reshape(bf16[24,768]{1,0:T(8,128)(2,1)S(1)} %reduce.2) | data formatting | bytes 73728
  10.2 4.4 %all-to-all-start = ((bf16[4,2,2304]{2,1,0:T(2,128)(2,1)}), bf16[4,2,2304]{2,1,0:T(2,128)(2,1)S(1)}, u32[]{:S(2)}, u32[]{:S(2)}) async-start(bf16[4,2,2304]{2,1,0:T(2,128)(2,1)} %reshape.39), calls=%async_computation | async-start | bytes 73728 | tf_op jit(solution)/shard_map/all_to_all | solution.py:84
  14.7 0.7 %copy-done.2 = bf16[32,4]{0,1:T(4,128)(2,1)S(1)} copy-done((bf16[32,4]{0,1:T(4,128)(2,1)S(1)}, bf16[32,4]{0,1:T(4,128)(2,1)}, u32[]{:S(2)}) %copy-start.2) | copy-done | bytes 280
  15.4 0.1 copy.15
  15.5 0.6 %gather_fusion = bf16[32,4]{1,0:T(8,128)(2,1)S(1)} fusion(bf16[32,4]{1,0:T(8,128)(2,1)S(1)} %copy.15, s32[1024]{0:T(1024)S(1)} %pad_clamp_fusion), kind=kCustom, calls=%fused_computation | custom fusion | bytes 640 | tf_op jit(solution)/shard_map/jit(_take)/gather | solution.py:82
  16.1 2.4 %all-to-all-done = bf16[4,2,2304]{2,1,0:T(2,128)(2,1)S(1)} async-done(((bf16[4,2,2304]{2,1,0:T(2,128)(2,1)}), bf16[4,2,2304]{2,1,0:T(2,128)(2,1)S(1)}, u32[]{:S(2)}, u32[]{:S(2)}) %all-to-all-start) | async-done | bytes 36896 | tf_op jit(solution)/shard_map/all_to_all | solution.py:84
  18.6 0.2 bitcast_reduce_fusion
  18.8 2.0 %collective-permute-start = (bf16[4,4608]{1,0:T(4,128)(2,1)S(1)}, bf16[4,4608]{1,0:T(4,128)(2,1)S(1)}, u32[]{:S(2)}, u32[]{:S(2)}) collective-permute-start(bf16[4,4608]{1,0:T(4,128)(2,1)S(1)} %reshape.28), channel_id=1, source_target_pairs={{0,4},{4,8},{8,12},{12,16},{16,20},{20,24},{24,28},{28,0},{1,5},{5... | collective-permute-start | bytes 110600 | tf_op jit(solution)/shard_map/ppermute | solution.py:24
  20.8 3.1 %collective-permute-start.1 = (bf16[4,4608]{1,0:T(4,128)(2,1)S(1)}, bf16[4,4608]{1,0:T(4,128)(2,1)S(1)}, u32[]{:S(2)}, u32[]{:S(2)}) collective-permute-start(bf16[4,4608]{1,0:T(4,128)(2,1)S(1)} %reshape.28), channel_id=1, source_target_pairs={{0,28},{4,0},{8,4},{12,8},{16,12},{20,16},{24,20},{28,24},{1,29},{... | collective-permute-start | bytes 110600 | tf_op jit(solution)/shard_map/ppermute | solution.py:29
  24.0 1.8 %collective-permute-done = bf16[4,4608]{1,0:T(4,128)(2,1)S(1)} collective-permute-done((bf16[4,4608]{1,0:T(4,128)(2,1)S(1)}, bf16[4,4608]{1,0:T(4,128)(2,1)S(1)}, u32[]{:S(2)}, u32[]{:S(2)}) %collective-permute-start) | collective-permute-done | bytes 36896 | tf_op jit(solution)/shard_map/ppermute | solution.py:24
  25.8 4.8 %collective-permute-start.3 = (bf16[4,4608]{1,0:T(4,128)(2,1)S(1)}, bf16[4,4608]{1,0:T(4,128)(2,1)S(1)}, u32[]{:S(2)}, u32[]{:S(2)}) collective-permute-start(bf16[4,4608]{1,0:T(4,128)(2,1)S(1)} %collective-permute-done.1), channel_id=1, source_target_pairs={{0,28},{4,0},{8,4},{12,8},{16,12},{20,16},{24,20},{28,24},{1,29},{... | collective-permute-start | bytes 110600 | tf_op jit(solution)/shard_map/ppermute | solution.py:29
  30.6 1.8 %collective-permute-done.2 = bf16[4,4608]{1,0:T(4,128)(2,1)S(1)} collective-permute-done((bf16[4,4608]{1,0:T(4,128)(2,1)S(1)}, bf16[4,4608]{1,0:T(4,128)(2,1)S(1)}, u32[]{:S(2)}, u32[]{:S(2)}) %collective-permute-start.2) | collective-permute-done | bytes 36896 | tf_op jit(solution)/shard_map/ppermute | solution.py:24
  32.4 4.8 %collective-permute-start.5 = (bf16[4,4608]{1,0:T(4,128)(2,1)S(1)}, bf16[4,4608]{1,0:T(4,128)(2,1)S(1)}, u32[]{:S(2)}, u32[]{:S(2)}) collective-permute-start(bf16[4,4608]{1,0:T(4,128)(2,1)S(1)} %collective-permute-done.3), channel_id=1, source_target_pairs={{0,28},{4,0},{8,4},{12,8},{16,12},{20,16},{24,20},{28,24},{1,29},{... | collective-permute-start | bytes 110600 | tf_op jit(solution)/shard_map/ppermute | solution.py:29
  37.3 1.8 %collective-permute-done.4 = bf16[4,4608]{1,0:T(4,128)(2,1)S(1)} collective-permute-done((bf16[4,4608]{1,0:T(4,128)(2,1)S(1)}, bf16[4,4608]{1,0:T(4,128)(2,1)S(1)}, u32[]{:S(2)}, u32[]{:S(2)}) %collective-permute-start.4) | collective-permute-done | bytes 36896 | tf_op jit(solution)/shard_map/ppermute | solution.py:24
  39.2 6.6 %collective-permute-done.6 = bf16[4,4608]{1,0:T(4,128)(2,1)S(1)} collective-permute-done((bf16[4,4608]{1,0:T(4,128)(2,1)S(1)}, bf16[4,4608]{1,0:T(4,128)(2,1)S(1)}, u32[]{:S(2)}, u32[]{:S(2)}) %collective-permute-start.6) | collective-permute-done | bytes 36896 | tf_op jit(solution)/shard_map/ppermute | solution.py:24
  45.8 0.9 %convolution_convert_fusion = bf16[4,4608]{1,0:T(4,128)(2,1)} fusion(bf16[32,4608]{1,0:T(8,128)(2,1)S(1)} %constant_dynamic-update-slice_fusion, bf16[32,4]{1,0:T(8,128)(2,1)S(1)} %gather_fusion, pred[32]{0:T(512)(128)(4,1)S(1)} %compare_and_fusion), kind=kOutput, calls=%fused_computation.1 | convolution fusion | flops 1198208 | bytes 332064 | tf_op jit(solution)/shard_map/dot_general | solution.py:87
  (79 shorter events, 2.5 us)
Async XLA Ops:
  0.0 1.1 %copy-start = (f32[1,24,768]{2,1,0:T(8,128)S(1)}, f32[1,24,768]{2,1,0:T(8,128)}, u32[]{:S(2)}) copy-start(f32[1,24,768]{2,1,0:T(8,128)} %param.5) | copy-start | bytes 221188
  2.1 0.9 %copy-start.1 = (s32[24,768]{1,0:T(8,128)S(1)}, s32[24,768]{1,0:T(8,128)}, u32[]{:S(2)}) copy-start(s32[24,768]{1,0:T(8,128)} %param.6) | copy-start | bytes 221188
  2.1 0.9 %copy-start.3 = (f32[8]{0:T(128)S(1)}, f32[8]{0:T(128)}, u32[]{:S(2)}) copy-start(f32[8]{0:T(128)} %param.7) | copy-start | bytes 100
  10.2 4.4 %copy-start.4 = (s32[32]{0:T(128)S(1)}, s32[32]{0:T(128)}, u32[]{:S(2)}) copy-start(s32[32]{0:T(128)} %param.9) | copy-start | bytes 388
  10.2 8.4 %all-to-all-start = ((bf16[4,2,2304]{2,1,0:T(2,128)(2,1)}), bf16[4,2,2304]{2,1,0:T(2,128)(2,1)S(1)}, u32[]{:S(2)}, u32[]{:S(2)}) async-start(bf16[4,2,2304]{2,1,0:T(2,128)(2,1)} %reshape.39), calls=%async_computation | async-start | bytes 73728 | tf_op jit(solution)/shard_map/all_to_all | solution.py:84
  14.7 0.7 %copy-start.2 = (bf16[32,4]{0,1:T(4,128)(2,1)S(1)}, bf16[32,4]{0,1:T(4,128)(2,1)}, u32[]{:S(2)}) copy-start(bf16[32,4]{0,1:T(4,128)(2,1)} %param.8) | copy-start | bytes 772
  18.8 7.0 %collective-permute-start = (bf16[4,4608]{1,0:T(4,128)(2,1)S(1)}, bf16[4,4608]{1,0:T(4,128)(2,1)S(1)}, u32[]{:S(2)}, u32[]{:S(2)}) collective-permute-start(bf16[4,4608]{1,0:T(4,128)(2,1)S(1)} %reshape.28), channel_id=1, source_target_pairs={{0,4},{4,8},{8,12},{12,16},{16,20},{20,24},{24,28},{28,0},{1,5},{5... | collective-permute-start | bytes 110600 | tf_op jit(solution)/shard_map/ppermute | solution.py:24
  20.8 5.0 %collective-permute-start.1 = (bf16[4,4608]{1,0:T(4,128)(2,1)S(1)}, bf16[4,4608]{1,0:T(4,128)(2,1)S(1)}, u32[]{:S(2)}, u32[]{:S(2)}) collective-permute-start(bf16[4,4608]{1,0:T(4,128)(2,1)S(1)} %reshape.28), channel_id=1, source_target_pairs={{0,28},{4,0},{8,4},{12,8},{16,12},{20,16},{24,20},{28,24},{1,29},{... | collective-permute-start | bytes 110600 | tf_op jit(solution)/shard_map/ppermute | solution.py:29
  25.8 6.7 %collective-permute-start.2 = (bf16[4,4608]{1,0:T(4,128)(2,1)S(1)}, bf16[4,4608]{1,0:T(4,128)(2,1)S(1)}, u32[]{:S(2)}, u32[]{:S(2)}) collective-permute-start(bf16[4,4608]{1,0:T(4,128)(2,1)S(1)} %collective-permute-done), channel_id=1, source_target_pairs={{0,4},{4,8},{8,12},{12,16},{16,20},{20,24},{24,28},{28,0},{1,5},{5... | collective-permute-start | bytes 110600 | tf_op jit(solution)/shard_map/ppermute | solution.py:24
  25.8 6.7 %collective-permute-start.3 = (bf16[4,4608]{1,0:T(4,128)(2,1)S(1)}, bf16[4,4608]{1,0:T(4,128)(2,1)S(1)}, u32[]{:S(2)}, u32[]{:S(2)}) collective-permute-start(bf16[4,4608]{1,0:T(4,128)(2,1)S(1)} %collective-permute-done.1), channel_id=1, source_target_pairs={{0,28},{4,0},{8,4},{12,8},{16,12},{20,16},{24,20},{28,24},{1,29},{... | collective-permute-start | bytes 110600 | tf_op jit(solution)/shard_map/ppermute | solution.py:29
  32.4 6.7 %collective-permute-start.4 = (bf16[4,4608]{1,0:T(4,128)(2,1)S(1)}, bf16[4,4608]{1,0:T(4,128)(2,1)S(1)}, u32[]{:S(2)}, u32[]{:S(2)}) collective-permute-start(bf16[4,4608]{1,0:T(4,128)(2,1)S(1)} %collective-permute-done.2), channel_id=1, source_target_pairs={{0,4},{4,8},{8,12},{12,16},{16,20},{20,24},{24,28},{28,0},{1,5},{5... | collective-permute-start | bytes 110600 | tf_op jit(solution)/shard_map/ppermute | solution.py:24
  32.4 6.7 %collective-permute-start.5 = (bf16[4,4608]{1,0:T(4,128)(2,1)S(1)}, bf16[4,4608]{1,0:T(4,128)(2,1)S(1)}, u32[]{:S(2)}, u32[]{:S(2)}) collective-permute-start(bf16[4,4608]{1,0:T(4,128)(2,1)S(1)} %collective-permute-done.3), channel_id=1, source_target_pairs={{0,28},{4,0},{8,4},{12,8},{16,12},{20,16},{24,20},{28,24},{1,29},{... | collective-permute-start | bytes 110600 | tf_op jit(solution)/shard_map/ppermute | solution.py:29
  39.1 6.7 %collective-permute-start.6 = (bf16[4,4608]{1,0:T(4,128)(2,1)S(1)}, bf16[4,4608]{1,0:T(4,128)(2,1)S(1)}, u32[]{:S(2)}, u32[]{:S(2)}) collective-permute-start(bf16[4,4608]{1,0:T(4,128)(2,1)S(1)} %collective-permute-done.4), channel_id=1, source_target_pairs={{0,4},{4,8},{8,12},{12,16},{16,20},{20,24},{24,28},{28,0},{1,5},{5... | collective-permute-start | bytes 110600 | tf_op jit(solution)/shard_map/ppermute | solution.py:24
